TPU v7x, 512 devices: a whole 4x4x16 slice. The times are simulated.
512 devices in a mesh: dp: 32 (over y, x, core), tensor: 16 (over z).
Axes of the slice: x: 4, y: 4, z: 16, core: 2. Of those that a mesh axis runs over, the one named last changes fastest.
Arguments:
- x_tokens: bfloat16 [2048, 8192], P('dp', 'tensor'), may hold values from -6 to 6
- sign_bits: int32 [8192], P('tensor'), may hold values from 0 to 1
- weight: bfloat16 [8192, 28672], P('tensor', 'dp'), may hold values from -0.0625 to 0.0625
- upstream: bfloat16 [2048, 28672], P('tensor', 'dp'), may hold values from -0.125 to 0.125
Outputs:
- projected: bfloat16 [2048, 28672], P('tensor', 'dp')
- weight_grad: float32 [8192, 28672], P('tensor', 'dp')
All inputs are finite; a program needn't handle non-finite values.
Results may differ from a plain program's by a relative error of at most 0.028.
Values may be sent and summed in bfloat16 or wider, within the bound.
A program may use at most 64 MiB of HBM per device.

v0:
```python
import math

import jax
import jax.numpy as jnp
from jax import lax
from jax.sharding import PartitionSpec as P


def partner_2(block, axis, stride):
    count = lax.axis_size(axis)
    route = []
    for low in range(count):
        high = low | 1 << stride
        if high != low and high < count:
            route += [(low, high), (high, low)]
    return lax.ppermute(block, axis, route)


def hadamard(order):
    row_ids = jnp.arange(order, dtype=jnp.int32)[:, None]
    col_ids = jnp.arange(order, dtype=jnp.int32)[None, :]
    common = row_ids & col_ids
    parity = jnp.zeros((order, order), jnp.int32)
    for section_bit in range(max(order.bit_length() - 1, 0)):
        parity = parity + (common >> section_bit & 1)
    return (1 - 2 * (parity % 2)).astype(jnp.float32)


def per_device(x_tokens, sign_bits, weight, upstream):
    panel_width = x_tokens.shape[1]
    groups = lax.axis_size("tensor")
    factor = 1.0 / math.sqrt(panel_width * groups)
    column_sign = (1 - 2 * sign_bits).astype(jnp.bfloat16)
    signed = x_tokens * column_sign[None, :]
    partial_rot = jnp.dot(
        signed, hadamard(panel_width).astype(jnp.bfloat16), preferred_element_type=jnp.float32
    )
    current = partial_rot
    position = lax.axis_index("tensor")
    for section_bit in range(groups.bit_length() - 1):
        partner = partner_2(current.astype(jnp.bfloat16), "tensor", section_bit).astype(
            current.dtype
        )
        upper_half = position >> section_bit & 1 == 1
        current = jnp.where(upper_half, partner - current, current + partner)
    quantized = (current * factor).astype(jnp.bfloat16)
    gathered = lax.all_gather(quantized, "dp", axis=0, tiled=True)
    selected = gathered
    projected = lax.psum_scatter(
        jnp.dot(selected, weight, preferred_element_type=jnp.float32).astype(jnp.bfloat16),
        "tensor",
        scatter_dimension=0,
        tiled=True,
    )
    selected = gathered
    weight_grad = lax.dot_general(
        selected,
        lax.all_gather(upstream, "tensor", axis=0, tiled=True),
        (((0,), (0,)), ((), ())),
        preferred_element_type=jnp.float32,
    )
    return (projected, weight_grad)


def solution(mesh):
    in_specs = (P("dp", "tensor"), P("tensor"), P("tensor", "dp"), P("tensor", "dp"))
    out_specs = (P("tensor", "dp"), P("tensor", "dp"))
    return jax.shard_map(
        per_device, mesh=mesh, in_specs=in_specs, out_specs=out_specs, check_vma=False
    )
```

profile of v0, /device:TPU:6, one launch (start us, length us, event | category | flops | bytes accessed | tf_op | source)
XLA Modules:
  0.0 280.2 jit_solution(17460488500459708254)
XLA Ops:
  7.2 0.0 copy-start
  7.2 0.0 all-gather.3.cloned.1.call-start
  7.2 0.8 subtract_convert_fusion
  8.0 2.5 fusion.28
  10.5 3.8 %collective-permute-start = (bf16[64,512]{1,0:T(8,128)(2,1)S(1)}, bf16[64,512]{1,0:T(8,128)(2,1)S(1)}, u32[]{:S(2)}, u32[]{:S(2)}) collective-permute-start(bf16[64,512]{1,0:T(8,128)(2,1)S(1)} %get-tuple-element.4), channel_id=1, source_target_pairs={{0,1},{1,0},{2,3},{3,2},{4,5},{5,4},{6,7},{7,6},{8,9},{9,8},{10,11... | collective-permute-start | bytes 196616 | tf_op jit(solution)/shard_map/ppermute | solution.py:16
  14.4 2.3 collective-permute-done
  16.7 5.2 %collective-permute-start.1 = (bf16[64,512]{1,0:T(8,128)(2,1)S(1)}, bf16[64,512]{1,0:T(8,128)(2,1)S(1)}, u32[]{:S(2)}, u32[]{:S(2)}) collective-permute-start(bf16[64,512]{1,0:T(8,128)(2,1)S(1)} %fusion.14), channel_id=1, source_target_pairs={{0,2},{2,0},{1,3},{3,1},{4,6},{6,4},{5,7},{7,5},{8,10},{10,8},{9,1... | collective-permute-start | bytes 196616 | tf_op jit(solution)/shard_map/ppermute | solution.py:16
  21.9 2.3 collective-permute-done.1
  24.2 9.1 %collective-permute-start.2 = (bf16[64,512]{1,0:T(8,128)(2,1)S(1)}, bf16[64,512]{1,0:T(8,128)(2,1)S(1)}, u32[]{:S(2)}, u32[]{:S(2)}) collective-permute-start(bf16[64,512]{1,0:T(8,128)(2,1)S(1)} %get-tuple-element.2), channel_id=1, source_target_pairs={{0,4},{4,0},{1,5},{5,1},{2,6},{6,2},{3,7},{7,3},{8,12},{12,8},{9,1... | collective-permute-start | bytes 196616 | tf_op jit(solution)/shard_map/ppermute | solution.py:16
  33.3 2.3 collective-permute-done.2
  35.7 16.6 %collective-permute-start.3 = (bf16[64,512]{1,0:T(8,128)(2,1)S(1)}, bf16[64,512]{1,0:T(8,128)(2,1)S(1)}, u32[]{:S(2)}, u32[]{:S(2)}) collective-permute-start(bf16[64,512]{1,0:T(8,128)(2,1)S(1)} %fusion.13), channel_id=1, source_target_pairs={{0,8},{8,0},{1,9},{9,1},{2,10},{10,2},{3,11},{11,3},{4,12},{12,4},... | collective-permute-start | bytes 196616 | tf_op jit(solution)/shard_map/ppermute | solution.py:16
  52.3 3.6 %collective-permute-done.3 = bf16[64,512]{1,0:T(8,128)(2,1)S(1)} collective-permute-done((bf16[64,512]{1,0:T(8,128)(2,1)S(1)}, bf16[64,512]{1,0:T(8,128)(2,1)S(1)}, u32[]{:S(2)}, u32[]{:S(2)}) %collective-permute-start.3) | collective-permute-done | bytes 65568 | tf_op jit(solution)/shard_map/ppermute | solution.py:16
  55.9 0.7 fusion.12
  56.6 0.0 all-gather.3.cloned.1.call-update
  56.6 0.0 all-gather.5.cloned.1.call-start
  56.6 0.7 all-gather.5.cloned.1.call-update
  57.3 0.0 reduce-scatter.2.cloned.1.call-start
  57.4 58.0 %all-gather.3.cloned.1.call-done = bf16[2048,512]{1,0:T(8,128)(2,1)} async-done(((bf16[64,512]{1,0:T(8,128)(2,1)}), bf16[2048,512]{1,0:T(8,128)(2,1)}) %all-gather.3.cloned.1.call-update) | async-done | bytes 2097168 | tf_op jit(solution)/shard_map/all_gather | solution.py:47
  115.4 0.0 copy-done
  115.4 5.8 %convolution_convert_fusion = bf16[2048,896]{1,0:T(8,128)(2,1)} fusion(bf16[2048,512]{1,0:T(8,128)(2,1)} %all-gather.3.cloned.1.call-done, bf16[512,896]{1,0:T(8,128)(2,1)S(1)} %copy-done), kind=kOutput, calls=%fused_computation | convolution fusion | flops 1880883200 | bytes 6684672 | tf_op jit(solution)/shard_map/dot_general | solution.py:50
  121.2 0.0 copy-start.1
  121.2 0.0 reduce-scatter.2.cloned.1.call-update
  121.2 73.5 %all-gather.5.cloned.1.call-done = bf16[2048,896]{1,0:T(8,128)(2,1)} async-done(((bf16[128,896]{1,0:T(8,128)(2,1)}), bf16[2048,896]{1,0:T(8,128)(2,1)}) %all-gather.5.cloned.1.call-update) | async-done | bytes 3670032 | tf_op jit(solution)/shard_map/all_gather | solution.py:58
  194.8 0.0 copy-done.1
  194.8 5.6 %fusion.29 = f32[512,896]{1,0:T(8,128)} fusion(bf16[2048,512]{1,0:T(8,128)(2,1)S(1)} %copy-done.1, bf16[2048,896]{1,0:T(8,128)(2,1)} %all-gather.5.cloned.1.call-done), kind=kOutput, calls=%fused_computation.40 | convolution fusion | flops 1879048192 | bytes 7602176 | tf_op jit(solution)/shard_map/dot_general | solution.py:56
  200.4 73.3 %reduce-scatter.2.cloned.1.call-done = bf16[128,896]{1,0:T(8,128)(2,1)} async-done(((bf16[2048,896]{1,0:T(8,128)(2,1)}), bf16[128,896]{1,0:T(8,128)(2,1)}) %reduce-scatter.2.cloned.1.call-update) | async-done | bytes 229392 | tf_op jit(solution)/shard_map/reduce_scatter | solution.py:49
  (3 shorter events, 0.1 us)
Async XLA Ops:
  7.2 108.2 %copy-start = (bf16[512,896]{1,0:T(8,128)(2,1)S(1)}, bf16[512,896]{1,0:T(8,128)(2,1)}, u32[]{:S(2)}) copy-start(bf16[512,896]{1,0:T(8,128)(2,1)} %param.6) | copy-start | bytes 2752516
  7.2 108.2 %all-gather.3.cloned.1.call-start = ((), (), s32[]{:S(2)}) async-start(), calls=%async_computation.1 | async-start | bytes 2162688 | tf_op jit(solution)/shard_map/all_gather | solution.py:47
  10.5 6.2 %collective-permute-start = (bf16[64,512]{1,0:T(8,128)(2,1)S(1)}, bf16[64,512]{1,0:T(8,128)(2,1)S(1)}, u32[]{:S(2)}, u32[]{:S(2)}) collective-permute-start(bf16[64,512]{1,0:T(8,128)(2,1)S(1)} %get-tuple-element.4), channel_id=1, source_target_pairs={{0,1},{1,0},{2,3},{3,2},{4,5},{5,4},{6,7},{7,6},{8,9},{9,8},{10,11... | collective-permute-start | bytes 196616 | tf_op jit(solution)/shard_map/ppermute | solution.py:16
  16.7 7.5 %collective-permute-start.1 = (bf16[64,512]{1,0:T(8,128)(2,1)S(1)}, bf16[64,512]{1,0:T(8,128)(2,1)S(1)}, u32[]{:S(2)}, u32[]{:S(2)}) collective-permute-start(bf16[64,512]{1,0:T(8,128)(2,1)S(1)} %fusion.14), channel_id=1, source_target_pairs={{0,2},{2,0},{1,3},{3,1},{4,6},{6,4},{5,7},{7,5},{8,10},{10,8},{9,1... | collective-permute-start | bytes 196616 | tf_op jit(solution)/shard_map/ppermute | solution.py:16
  24.2 11.4 %collective-permute-start.2 = (bf16[64,512]{1,0:T(8,128)(2,1)S(1)}, bf16[64,512]{1,0:T(8,128)(2,1)S(1)}, u32[]{:S(2)}, u32[]{:S(2)}) collective-permute-start(bf16[64,512]{1,0:T(8,128)(2,1)S(1)} %get-tuple-element.2), channel_id=1, source_target_pairs={{0,4},{4,0},{1,5},{5,1},{2,6},{6,2},{3,7},{7,3},{8,12},{12,8},{9,1... | collective-permute-start | bytes 196616 | tf_op jit(solution)/shard_map/ppermute | solution.py:16
  35.7 20.2 %collective-permute-start.3 = (bf16[64,512]{1,0:T(8,128)(2,1)S(1)}, bf16[64,512]{1,0:T(8,128)(2,1)S(1)}, u32[]{:S(2)}, u32[]{:S(2)}) collective-permute-start(bf16[64,512]{1,0:T(8,128)(2,1)S(1)} %fusion.13), channel_id=1, source_target_pairs={{0,8},{8,0},{1,9},{9,1},{2,10},{10,2},{3,11},{11,3},{4,12},{12,4},... | collective-permute-start | bytes 196616 | tf_op jit(solution)/shard_map/ppermute | solution.py:16
  56.6 138.2 %all-gather.5.cloned.1.call-start = ((), (), s32[]{:S(2)}) async-start(), calls=%async_computation.3 | async-start | bytes 3899392 | tf_op jit(solution)/shard_map/all_gather | solution.py:58
  57.3 216.4 %reduce-scatter.2.cloned.1.call-start = ((), (), s32[]{:S(2)}) async-start(), calls=%async_computation.2 | async-start | bytes 3899392 | tf_op jit(solution)/shard_map/reduce_scatter | solution.py:49
  121.2 73.6 %copy-start.1 = (bf16[2048,512]{1,0:T(8,128)(2,1)S(1)}, bf16[2048,512]{1,0:T(8,128)(2,1)}, u32[]{:S(2)}) copy-start(bf16[2048,512]{1,0:T(8,128)(2,1)} %all-gather.3.cloned.1.call-done) | copy-start | bytes 6291460
Sparse Core Ops, SparseCore 0:
  56.7 58.6 all-gather.2
  117.5 77.2 all-gather.4
  198.2 75.4 reduce-scatter.1
where the time goes:
time: 281 us; the launch traced here: 280 us
  waiting for transfers between devices  216 us (77%)
  starting transfers between devices  34.9 us (12%)
  matrix products  13.9 us (5%)
  between operations  13.8 us (5%)
    all_gather x1, waiting for transfers between devices, per_device(): lax.all_gather(upstream, 'tensor', axis=0, tiled=True)  73.5 us
    reduce_scatter x1, waiting for transfers between devices, per_device(): lax.psum_scatter(jnp.dot(selected, weight, preferred_element_type=jnp.flo...  73.3 us
    all_gather x1, waiting for transfers between devices, per_device(): gathered = lax.all_gather(quantized, 'dp', axis=0, tiled=True)  58 us
    ppermute x4, starting transfers between devices, partner_2(): return lax.ppermute(block, axis, route)  34.7 us
    ppermute x4, waiting for transfers between devices, partner_2(): return lax.ppermute(block, axis, route)  10.5 us
    dot_general x1, matrix products, per_device(): jnp.dot(selected, weight, preferred_element_type=jnp.float32)  5.78 us
  transfers between devices with their start and end apart: 7, of which 7 were waited for; matrix products, arithmetic and copies ran while one was open for 4% of the time, Pallas kernels for 0%

commit v1 on v0

v1 whole, which is shorter than its diff:
```python
import math

import jax
import jax.numpy as jnp
from jax import lax
from jax.experimental import pallas as pl
from jax.experimental.pallas import tpu as pltpu
from jax.sharding import PartitionSpec as P

MESH = pl.DeviceIdType.MESH
F32 = jnp.float32
BF16 = jnp.bfloat16
NZ = 16
NX = 4
NY = 4
SUB = 2


def hadamard_128():
    rows = lax.broadcasted_iota(jnp.int32, (128, 128), 0)
    cols = lax.broadcasted_iota(jnp.int32, (128, 128), 1)
    bits = rows & cols
    bits = bits ^ (bits >> 4)
    bits = bits ^ (bits >> 2)
    bits = bits ^ (bits >> 1)
    return (1 - 2 * (bits & 1)).astype(F32).astype(BF16)


def butterfly(values):
    values = list(values)
    stride = 1
    while stride < len(values):
        for low in range(len(values)):
            if not low & stride:
                a, b = values[low], values[low | stride]
                values[low], values[low | stride] = a + b, a - b
        stride *= 2
    return values


def kernel(
    x_ref, sign_ref, w_hbm, u_hbm, proj_ref, grad_ref,
    inner, recv1, send2, q, qt, w, uall, part, rbuf, sbuf,
    loc_sem, a1_send, a1_recv, a2_send, a2_recv,
    x_send, x_recv, y_send, y_recv, c_send, c_recv,
    ag_send, ag_recv, rs_send, rs_recv,
):
    me = lax.axis_index("tensor")
    dp = lax.axis_index("dp")
    core = lax.rem(dp, 2)
    chip = lax.div(dp, 2)
    xx = lax.rem(chip, NX)
    yy = lax.div(chip, NX)
    half = q.shape[1] // NZ
    quarter = half * NX

    def z_dev(shift):
        return {"tensor": lax.rem(me + shift + NZ, NZ)}

    def x_dev(shift):
        return {"dp": (yy * NX + lax.rem(xx + shift, NX)) * 2 + core}

    def y_dev(shift):
        return {"dp": (lax.rem(yy + shift, NY) * NX + xx) * 2 + core}

    partner = {"dp": chip * 2 + 1 - core}

    w_copy = pltpu.make_async_copy(w_hbm, w, loc_sem.at[0])
    w_copy.start()
    own_rows = pl.ds(pl.multiple_of(me * half, half), half)
    u_copies = []
    for h in range(2):
        cp = pltpu.make_async_copy(
            u_hbm.at[pl.ds(h * half, half)], uall.at[h, own_rows], loc_sem.at[1 + h]
        )
        cp.start()
        u_copies.append(cp)

    barrier = pltpu.get_barrier_semaphore()

    def greet(device):
        pl.semaphore_signal(barrier, inc=1, device_id=device, device_id_type=MESH)

    for k in range(1, NZ):
        greet(z_dev(k))
    for k in range(1, NX):
        greet(x_dev(k))
    for k in range(1, NY):
        greet(y_dev(k))
    greet(partner)

    had = hadamard_128()
    column_sign = (1 - 2 * sign_ref[...]).astype(F32)
    signed = (x_ref[...].astype(F32) * column_sign).astype(BF16)
    groups = butterfly(
        [
            jnp.dot(signed[:, g * 128 : (g + 1) * 128], had, preferred_element_type=F32)
            for g in range(4)
        ]
    )
    for a in range(4):
        for g in range(4):
            inner[a * 4 + g] = groups[g][a * 16 : (a + 1) * 16].astype(BF16)

    pl.semaphore_wait(barrier, NZ - 1 + NX - 1 + NY - 1 + 1)

    pending = []

    def send(src, dst, s_sem, r_sem, device):
        cp = pltpu.make_async_remote_copy(
            src_ref=src, dst_ref=dst, send_sem=s_sem, recv_sem=r_sem,
            device_id=device, device_id_type=MESH,
        )
        cp.start()
        pending.append(cp)

    def arrived(ref, sem):
        pltpu.make_async_remote_copy(
            src_ref=ref, dst_ref=ref, send_sem=sem, recv_sem=sem,
            device_id=partner, device_id_type=MESH,
        ).wait_recv()

    for k in range(1, NZ):
        j = lax.rem(me + k, NZ)
        send(inner.at[j], recv1.at[me], a1_send.at[k], a1_recv.at[k], z_dev(k))

    SIGN = (1, -1)
    HOPS = ((8, 7), (7, 8))

    def gather_step(s):
        for h in range(2):
            for way in range(2):
                sign = SIGN[way]
                if s > 0 and s - 1 < HOPS[way][h]:
                    rows = pl.ds(
                        pl.multiple_of(lax.rem(me - sign * s + NZ, NZ) * half, half), half
                    )
                    arrived(uall.at[h, rows], ag_recv.at[way, h, s - 1])
                if s < HOPS[way][h]:
                    rows = pl.ds(
                        pl.multiple_of(lax.rem(me - sign * s + NZ, NZ) * half, half), half
                    )
                    src = u_hbm.at[pl.ds(h * half, half)] if s == 0 else uall.at[h, rows]
                    send(
                        src, uall.at[h, rows],
                        ag_send.at[way, h, s], ag_recv.at[way, h, s], z_dev(sign),
                    )

    gather_step(0)

    recv1[me] = inner[me]
    for k in range(1, NZ):
        arrived(recv1.at[lax.rem(me - k + NZ, NZ)], a1_recv.at[k])
    factor = 1.0 / math.sqrt(8192.0)
    rotated = butterfly([recv1[t].astype(F32) for t in range(NZ)])
    for s in range(NZ):
        send2[s] = (rotated[s] * factor).astype(BF16)

    q_own = pl.ds(pl.multiple_of(chip * half, half), half)
    tile_rows = pl.ds(pl.multiple_of(chip * half + lax.div(me, 4) * 16, 16), 16)
    tile_cols = pl.ds(pl.multiple_of(lax.rem(me, 4) * 128, 128), 128)
    for k in range(1, NZ):
        j = lax.rem(me + k, NZ)
        send(
            send2.at[j], q.at[core, tile_rows, tile_cols],
            a2_send.at[k], a2_recv.at[k], z_dev(k),
        )
    own_tile = pltpu.make_async_copy(
        send2.at[me], q.at[core, tile_rows, tile_cols], loc_sem.at[3]
    )
    own_tile.start()

    gather_step(1)

    own_tile.wait()
    for k in range(1, NZ):
        arrived(send2.at[0], a2_recv.at[k])

    for k in range(1, NX):
        send(q.at[core, q_own], q.at[core, q_own], x_send.at[k], x_recv.at[k], x_dev(k))

    gather_step(2)

    def chip_rows(y, x):
        return pl.ds(pl.multiple_of((y * NX + x) * half, half), half)

    def line_rows(y):
        return pl.ds(pl.multiple_of(y * quarter, quarter), quarter)

    for k in range(1, NX):
        arrived(q.at[core, chip_rows(yy, lax.rem(xx - k + NX, NX))], x_recv.at[k])
    own_line = q.at[core, line_rows(yy)]
    for k in range(1, NY):
        send(own_line, own_line, y_send.at[k], y_recv.at[k], y_dev(k))
    send(own_line, own_line, c_send.at[0], c_recv.at[0], partner)

    gather_step(3)

    for k in range(1, NY):
        line = q.at[core, line_rows(lax.rem(yy - k + NY, NY))]
        arrived(line, y_recv.at[k])
        send(line, line, c_send.at[k], c_recv.at[k], partner)

    w_copy.wait()

    def products(c):
        @pl.loop(0, NY)
        def _(y):
            rows = line_rows(y)
            block = q[c, rows]
            part[c, rows] = jnp.dot(block, w[...], preferred_element_type=F32)
            columns = pl.ds(
                pl.multiple_of((c * NY + y) * quarter, quarter), quarter
            )
            qt[:, columns] = block.T

    products(core)
    gather_step(4)
    for k in range(NY):
        arrived(q.at[1 - core, line_rows(lax.rem(yy - k + NY, NY))], c_recv.at[k])
    products(1 - core)

    piece = half // SUB

    def reduce_step(s):
        for h in range(2):
            for r in range(SUB):
                for way in range(2):
                    sign = SIGN[way]
                    first = 8 - HOPS[way][h]
                    if s < first:
                        continue
                    e = lax.rem(me + sign * (8 - s) + NZ, NZ)
                    rows = pl.ds(pl.multiple_of(e * half + r * piece, piece), piece)
                    cut = pl.ds(r * piece, piece)
                    mine = part[h, rows]
                    if s == first:
                        src = sbuf.at[way, h, cut]
                        src[...] = mine.astype(BF16)
                    else:
                        src = rbuf.at[way, h, s - 1, cut]
                        arrived(src, rs_recv.at[way, h, r, s - 1])
                        src[...] = (src[...].astype(F32) + mine).astype(BF16)
                    send(
                        src, rbuf.at[way, h, s, cut],
                        rs_send.at[way, h, r, s], rs_recv.at[way, h, r, s], z_dev(sign),
                    )

    def grad_tile(i):
        rows = pl.ds(i * 128, 128)
        n = q.shape[1]
        grad_ref[rows, :] = jnp.dot(
            qt[rows, 0:n], uall[0], preferred_element_type=F32
        ) + jnp.dot(qt[rows, n : 2 * n], uall[1], preferred_element_type=F32)

    reduce_step(0)
    gather_step(5)
    reduce_step(1)
    gather_step(6)
    reduce_step(2)
    gather_step(7)
    reduce_step(3)
    gather_step(8)
    for cp in u_copies:
        cp.wait()
    for s in range(4, 8):
        reduce_step(s)
        grad_tile(s - 4)

    for h in range(2):
        for r in range(SUB):
            cut = pl.ds(r * piece, piece)
            total = part[h, pl.ds(pl.multiple_of(me * half + r * piece, piece), piece)]
            for way in range(2):
                src = rbuf.at[way, h, 7, cut]
                arrived(src, rs_recv.at[way, h, r, 7])
                total = total + src[...].astype(F32)
            proj_ref[pl.ds(h * half + r * piece, piece), :] = total.astype(BF16)

    for cp in pending:
        cp.wait_send()


def per_device(x_tokens, sign_bits, weight, upstream):
    tokens, width = x_tokens.shape
    hidden = weight.shape[1]
    half = tokens
    every = NZ * half
    dma = pltpu.SemaphoreType.DMA
    vmem = pl.BlockSpec(memory_space=pltpu.VMEM)
    anywhere = pl.BlockSpec(memory_space=pl.ANY)
    return pl.pallas_call(
        kernel,
        out_shape=(
            jax.ShapeDtypeStruct((2 * half, hidden), BF16),
            jax.ShapeDtypeStruct((width, hidden), F32),
        ),
        in_specs=[vmem, vmem, anywhere, anywhere],
        out_specs=(vmem, vmem),
        scratch_shapes=[
            pltpu.VMEM((16, 16, 128), BF16),
            pltpu.VMEM((16, 16, 128), BF16),
            pltpu.VMEM((16, 16, 128), BF16),
            pltpu.VMEM((2, every, width), BF16),
            pltpu.VMEM((width, 2 * every), BF16),
            pltpu.VMEM((width, hidden), BF16),
            pltpu.VMEM((2, every, hidden), BF16),
            pltpu.VMEM((2, every, hidden), F32),
            pltpu.VMEM((2, 2, 8, half, hidden), BF16),
            pltpu.VMEM((2, 2, half, hidden), BF16),
            dma((4,)),
            dma((NZ,)), dma((NZ,)), dma((NZ,)), dma((NZ,)),
            dma((NX,)), dma((NX,)), dma((NY,)), dma((NY,)), dma((NY,)), dma((NY,)),
            dma((2, 2, 8)), dma((2, 2, 8)),
            dma((2, 2, SUB, 8)), dma((2, 2, SUB, 8)),
        ],
        compiler_params=pltpu.CompilerParams(
            collective_id=0, has_side_effects=True, vmem_limit_bytes=48 << 20
        ),
    )(x_tokens, sign_bits.reshape(1, width), weight, upstream)


def solution(mesh):
    in_specs = (P("dp", "tensor"), P("tensor"), P("tensor", "dp"), P("tensor", "dp"))
    out_specs = (P("tensor", "dp"), P("tensor", "dp"))
    return jax.shard_map(
        per_device, mesh=mesh, in_specs=in_specs, out_specs=out_specs, check_vma=False
    )
```

time: 281 us -> 114 us (0.41)
  waiting for transfers between devices: 216 us -> 0 us
  Pallas kernels: 0 us -> 107 us
  starting transfers between devices: 34.9 us -> 0 us
  matrix products: 13.9 us -> 0 us
  between operations: 13.8 us -> 0.65 us
  local copies, waits for them, and re-layouts: 0.01 us -> 5.55 us
    all_gather x2 -> x0, waiting for transfers between devices: 132 us -> none  [the longest x1 73.5 us: per_device(): lax.all_gather(upstream, 'tensor', axis=0, tiled=True)]
    pallas_call x0 -> x1, Pallas kernels: none -> 107 us  [per_device(): pl.pallas_call(kernel, out_shape=(jax.ShapeDtypeStruct((2 * half, hidden)...]
    reduce_scatter x1 -> x0, waiting for transfers between devices: 73.3 us -> none  [per_device(): lax.psum_scatter(jnp.dot(selected, weight, preferred_element_type=jnp.flo...]
    ppermute x4 -> x0, starting transfers between devices: 34.7 us -> none  [partner_2(): return lax.ppermute(block, axis, route)]
    dot_general x3 -> x0, matrix products: 13.9 us -> none  [the longest x1 5.78 us: per_device(): jnp.dot(selected, weight, preferred_element_type=jnp.float32)]
    ppermute x4 -> x0, waiting for transfers between devices: 10.5 us -> none  [partner_2(): return lax.ppermute(block, axis, route)]
    unnamed x4 -> x10, local copies, waits for them, and re-layouts: 0.01 us -> 5.55 us
  transfers between devices with their start and end apart: 7 -> 0, of which waited for: 7 -> 0; matrix products, arithmetic and copies ran while one was open for 4% -> 0% of each run, Pallas kernels for 0% -> 0%
where the time goes in v1:
time: 114 us; the launch traced here: 113 us
  Pallas kernels  107 us (94%)
  local copies, waits for them, and re-layouts  5.55 us (5%)
    pallas_call x1, Pallas kernels, per_device(): pl.pallas_call(kernel, out_shape=(jax.ShapeDtypeStruct((2 * half, hidden)...  107 us
    unnamed x10, local copies, waits for them, and re-layouts  5.55 us

profile of v1, /device:TPU:6, one launch (start us, length us, event | category | flops | bytes accessed | tf_op | source)
XLA Modules:
  0.0 112.8 jit_solution(7398703873898716041)
XLA Ops:
  0.6 0.0 copy-start
  0.6 1.2 %copy-done = bf16[512,896]{1,0:T(8,128)(2,1)S(1)} copy-done((bf16[512,896]{1,0:T(8,128)(2,1)S(1)}, bf16[512,896]{1,0:T(8,128)(2,1)}, u32[]{:S(2)}) %copy-start) | copy-done | bytes 917528
  1.8 0.0 copy-start.1
  1.8 0.9 copy-done.1
  2.7 0.0 copy-start.2
  2.8 0.8 copy-done.2
  3.6 0.0 copy-start.3
  3.6 0.7 copy-done.3
  4.3 106.6 %shard_map.59 = (bf16[128,896]{1,0:T(8,128)(2,1)S(1)}, f32[512,896]{1,0:T(8,128)S(1)}) custom-call(bf16[64,512]{1,0:T(8,128)(2,1)S(1)} %copy-done.2, s32[1,512]{1,0:T(1,128)S(1)} %bitcast.1, bf16[512,896]{1,0:T(8,128)(2,1)S(1)} %copy-done, bf16[128,896]{1,0:T(8,128)(2,1)S(1)} %copy-done.1), custom_call_target="tpu_custom_call" | custom-call | tf_op jit(solution)/shard_map/pallas_call | solution.py:292
  110.8 0.7 copy.8
  111.5 1.2 %copy.9 = f32[512,896]{1,0:T(8,128)} copy(f32[512,896]{1,0:T(8,128)S(1)} %get-tuple-element.5) | data formatting | bytes 3670016
Async XLA Ops:
  0.6 1.2 %copy-start = (bf16[512,896]{1,0:T(8,128)(2,1)S(1)}, bf16[512,896]{1,0:T(8,128)(2,1)}, u32[]{:S(2)}) copy-start(bf16[512,896]{1,0:T(8,128)(2,1)} %w_hbm.1) | copy-start | bytes 2752516
  1.8 0.9 copy-start.1
  2.7 0.8 copy-start.2
  3.6 0.7 copy-start.3

commit v2 on v1

v2 whole, which is shorter than its diff:
```python
import math

import jax
import jax.numpy as jnp
from jax import lax
from jax.experimental import pallas as pl
from jax.experimental.pallas import tpu as pltpu
from jax.sharding import PartitionSpec as P

MESH = pl.DeviceIdType.MESH
F32 = jnp.float32
BF16 = jnp.bfloat16
NZ = 16
NX = 4
NY = 4
PARTS = 2


def hadamard_128():
    rows = lax.broadcasted_iota(jnp.int32, (128, 128), 0)
    cols = lax.broadcasted_iota(jnp.int32, (128, 128), 1)
    bits = rows & cols
    bits = bits ^ (bits >> 4)
    bits = bits ^ (bits >> 2)
    bits = bits ^ (bits >> 1)
    return (1 - 2 * (bits & 1)).astype(F32).astype(BF16)


def butterfly(values):
    values = list(values)
    stride = 1
    while stride < len(values):
        for low in range(len(values)):
            if not low & stride:
                a, b = values[low], values[low | stride]
                values[low], values[low | stride] = a + b, a - b
        stride *= 2
    return values


def kernel(
    x_hbm, sign_hbm, w_hbm, u_hbm, proj_ref, grad_ref,
    x_ref, sign_ref, inner, recv1, send2, q, qt, w, uall, part, rbuf, sbuf,
    loc_sem, a1_send, a1_recv, a2_send, a2_recv,
    x_send, x_recv, y_send, y_recv, c_send, c_recv,
    ag_send, ag_recv, rs_send, rs_recv,
):
    me = lax.axis_index("tensor")
    dp = lax.axis_index("dp")
    core = lax.rem(dp, 2)
    chip = lax.div(dp, 2)
    xx = lax.rem(chip, NX)
    yy = lax.div(chip, NX)
    part_rows = q.shape[4]

    def z_dev(shift):
        return {"tensor": lax.rem(me + shift + NZ, NZ)}

    def x_dev(shift):
        return {"dp": (yy * NX + lax.rem(xx + shift, NX)) * 2 + core}

    def y_dev(shift):
        return {"dp": (lax.rem(yy + shift, NY) * NX + xx) * 2 + core}

    partner = {"dp": chip * 2 + 1 - core}

    x_copy = pltpu.make_async_copy(x_hbm, x_ref, loc_sem.at[4])
    x_copy.start()
    sign_copy = pltpu.make_async_copy(sign_hbm, sign_ref, loc_sem.at[5])
    sign_copy.start()
    w_copy = pltpu.make_async_copy(w_hbm, w, loc_sem.at[0])
    w_copy.start()
    u_copies = []
    for h in range(2):
        cp = pltpu.make_async_copy(u_hbm.at[h], uall.at[h, :, me], loc_sem.at[1 + h])
        cp.start()
        u_copies.append(cp)

    barrier = pltpu.get_barrier_semaphore()

    def greet(device):
        pl.semaphore_signal(barrier, inc=1, device_id=device, device_id_type=MESH)

    for k in range(1, NZ):
        greet(z_dev(k))
    for k in range(1, NX):
        greet(x_dev(k))
    for k in range(1, NY):
        greet(y_dev(k))
    greet(partner)

    had = hadamard_128()
    x_copy.wait()
    sign_copy.wait()
    column_sign = (1 - 2 * sign_ref[...]).astype(F32)
    signed = (x_ref[...].astype(F32) * column_sign).astype(BF16)
    groups = butterfly(
        [
            jnp.dot(signed[:, g * 128 : (g + 1) * 128], had, preferred_element_type=F32)
            for g in range(4)
        ]
    )
    for a in range(4):
        for g in range(4):
            inner[a * 4 + g] = groups[g][a * 16 : (a + 1) * 16].astype(BF16)

    pl.semaphore_wait(barrier, NZ - 1 + NX - 1 + NY - 1 + 1)

    pending = []

    def send(src, dst, s_sem, r_sem, device):
        cp = pltpu.make_async_remote_copy(
            src_ref=src, dst_ref=dst, send_sem=s_sem, recv_sem=r_sem,
            device_id=device, device_id_type=MESH,
        )
        cp.start()
        pending.append(cp)

    def arrived(ref, sem):
        pltpu.make_async_remote_copy(
            src_ref=ref, dst_ref=ref, send_sem=sem, recv_sem=sem,
            device_id=partner, device_id_type=MESH,
        ).wait_recv()

    for k in range(1, NZ):
        j = lax.rem(me + k, NZ)
        send(inner.at[j], recv1.at[me], a1_send.at[k], a1_recv.at[k], z_dev(k))

    SIGN = (1, -1)
    HOPS = ((8, 7), (7, 8))

    def gather_step(s):
        for h in range(2):
            for way in range(2):
                sign = SIGN[way]
                chunk = uall.at[h, :, lax.rem(me - sign * s + NZ, NZ)]
                if s > 0 and s - 1 < HOPS[way][h]:
                    arrived(chunk, ag_recv.at[way, h, s - 1])
                if s < HOPS[way][h]:
                    send(
                        u_hbm.at[h] if s == 0 else chunk, chunk,
                        ag_send.at[way, h, s], ag_recv.at[way, h, s], z_dev(sign),
                    )

    gather_step(0)

    recv1[me] = inner[me]
    for k in range(1, NZ):
        arrived(recv1.at[lax.rem(me - k + NZ, NZ)], a1_recv.at[k])
    factor = 1.0 / math.sqrt(8192.0)
    rotated = butterfly([recv1[t].astype(F32) for t in range(NZ)])
    for s in range(NZ):
        send2[s] = (rotated[s] * factor).astype(BF16)

    block = lax.div(me, 4)
    tile = q.at[
        core, lax.div(block, 2), yy, xx,
        pl.ds(pl.multiple_of(lax.rem(block, 2) * 16, 16), 16),
        pl.ds(pl.multiple_of(lax.rem(me, 4) * 128, 128), 128),
    ]
    for k in range(1, NZ):
        j = lax.rem(me + k, NZ)
        send(send2.at[j], tile, a2_send.at[k], a2_recv.at[k], z_dev(k))
    own_tile = pltpu.make_async_copy(send2.at[me], tile, loc_sem.at[3])
    own_tile.start()

    gather_step(1)

    own_tile.wait()
    for k in range(1, NZ):
        arrived(send2.at[0], a2_recv.at[k])

    def x_from(k):
        return lax.rem(xx - k + NX, NX)

    def y_from(k):
        return lax.rem(yy - k + NY, NY)

    for k in range(1, NX):
        own = q.at[core, 0, yy, xx]
        send(own, own, x_send.at[0, k], x_recv.at[0, k], x_dev(k))
        own = q.at[core, 1, yy, xx]
        send(own, own, y_send.at[0, k], y_recv.at[0, k], y_dev(k))

    gather_step(2)

    for k in range(1, NX):
        arrived(q.at[core, 0, yy, x_from(k)], x_recv.at[0, k])
        arrived(q.at[core, 1, y_from(k), xx], y_recv.at[0, k])
    line = q.at[core, 0, yy]
    column = q.at[core, 1, :, xx]
    for k in range(1, NX):
        send(line, line, y_send.at[1, k], y_recv.at[1, k], y_dev(k))
        send(column, column, x_send.at[1, k], x_recv.at[1, k], x_dev(k))
    send(line, line, c_send.at[0, 0], c_recv.at[0, 0], partner)
    send(column, column, c_send.at[1, 0], c_recv.at[1, 0], partner)

    gather_step(3)
    gather_step(4)

    for k in range(1, NX):
        line = q.at[core, 0, y_from(k)]
        arrived(line, y_recv.at[1, k])
        send(line, line, c_send.at[0, k], c_recv.at[0, k], partner)
        column = q.at[core, 1, :, x_from(k)]
        arrived(column, x_recv.at[1, k])
        send(column, column, c_send.at[1, k], c_recv.at[1, k], partner)

    w_copy.wait()

    def products(c):
        @pl.loop(0, 2 * PARTS)
        def _(i):
            p, ys = lax.div(i, 2), pl.ds(lax.rem(i, 2) * 2, 2)
            rows = 2 * NX * part_rows
            tokens = q[c, p, ys].reshape(rows, q.shape[5])
            part[c, p, ys] = jnp.dot(
                tokens, w[...], preferred_element_type=F32
            ).reshape(2, NX, part_rows, w.shape[1])
            at = pl.multiple_of((c * 2 * PARTS + i) * rows, rows)
            qt[:, pl.ds(at, rows)] = tokens.T

    products(core)
    gather_step(5)
    for k in range(NX):
        arrived(q.at[1 - core, 0, y_from(k)], c_recv.at[0, k])
        arrived(q.at[1 - core, 1, :, x_from(k)], c_recv.at[1, k])
    products(1 - core)

    def reduce_step(s):
        for h in range(2):
            for p in range(PARTS):
                for way in range(2):
                    sign = SIGN[way]
                    first = 8 - HOPS[way][h]
                    if s < first:
                        continue
                    e = lax.rem(me + sign * (8 - s) + NZ, NZ)
                    mine = part[h, p, lax.div(e, NX), lax.rem(e, NX)]
                    if s == first:
                        src = sbuf.at[way, h, p]
                        src[...] = mine.astype(BF16)
                    else:
                        src = rbuf.at[way, h, p, s - 1]
                        arrived(src, rs_recv.at[way, h, p, s - 1])
                        src[...] = (src[...].astype(F32) + mine).astype(BF16)
                    send(
                        src, rbuf.at[way, h, p, s],
                        rs_send.at[way, h, p, s], rs_recv.at[way, h, p, s], z_dev(sign),
                    )

    def grad_tile(i):
        rows = pl.ds(i * 128, 128)
        n = qt.shape[1] // 2
        grad_ref[rows, :] = jnp.dot(
            qt[rows, 0:n], uall[0].reshape(n, w.shape[1]), preferred_element_type=F32
        ) + jnp.dot(
            qt[rows, n : 2 * n], uall[1].reshape(n, w.shape[1]), preferred_element_type=F32
        )

    reduce_step(0)
    gather_step(6)
    reduce_step(1)
    gather_step(7)
    reduce_step(2)
    gather_step(8)
    for cp in u_copies:
        cp.wait()
    for s in range(3, 8):
        reduce_step(s)
        if s < 7:
            grad_tile(s - 3)

    for h in range(2):
        for p in range(PARTS):
            total = part[h, p, lax.div(me, NX), lax.rem(me, NX)]
            for way in range(2):
                src = rbuf.at[way, h, p, 7]
                arrived(src, rs_recv.at[way, h, p, 7])
                total = total + src[...].astype(F32)
            proj_ref[pl.ds((h * PARTS + p) * part_rows, part_rows), :] = total.astype(BF16)

    for cp in pending:
        cp.wait_send()


def in_hbm(array):
    return pltpu.with_memory_space_constraint(array, pltpu.HBM)


def per_device(x_tokens, sign_bits, weight, upstream):
    tokens, width = x_tokens.shape
    hidden = weight.shape[1]
    rows = tokens // PARTS
    every = 2 * NZ * tokens
    dma = pltpu.SemaphoreType.DMA
    vmem = pl.BlockSpec(memory_space=pltpu.VMEM)
    anywhere = pl.BlockSpec(memory_space=pl.ANY)
    return pl.pallas_call(
        kernel,
        out_shape=(
            jax.ShapeDtypeStruct((2 * tokens, hidden), BF16),
            jax.ShapeDtypeStruct((width, hidden), F32),
        ),
        in_specs=[anywhere] * 4,
        out_specs=(vmem, vmem),
        scratch_shapes=[
            pltpu.VMEM((tokens, width), BF16),
            pltpu.VMEM((1, width), jnp.int32),
            pltpu.VMEM((16, 16, 128), BF16),
            pltpu.VMEM((16, 16, 128), BF16),
            pltpu.VMEM((16, 16, 128), BF16),
            pltpu.VMEM((2, PARTS, NY, NX, rows, width), BF16),
            pltpu.VMEM((width, every), BF16),
            pltpu.VMEM((width, hidden), BF16),
            pltpu.VMEM((2, PARTS, NZ, rows, hidden), BF16),
            pltpu.VMEM((2, PARTS, NY, NX, rows, hidden), F32),
            pltpu.VMEM((2, 2, PARTS, 8, rows, hidden), BF16),
            pltpu.VMEM((2, 2, PARTS, rows, hidden), BF16),
            dma((6,)),
            dma((NZ,)), dma((NZ,)), dma((NZ,)), dma((NZ,)),
            dma((2, NX)), dma((2, NX)), dma((2, NY)), dma((2, NY)), dma((2, NX)), dma((2, NX)),
            dma((2, 2, 8)), dma((2, 2, 8)),
            dma((2, 2, PARTS, 8)), dma((2, 2, PARTS, 8)),
        ],
        compiler_params=pltpu.CompilerParams(
            collective_id=0, has_side_effects=True, vmem_limit_bytes=48 << 20
        ),
    )(
        in_hbm(x_tokens),
        in_hbm(sign_bits.reshape(1, width)),
        in_hbm(weight),
        in_hbm(upstream.reshape(2, PARTS, rows, hidden)),
    )


def solution(mesh):
    in_specs = (P("dp", "tensor"), P("tensor"), P("tensor", "dp"), P("tensor", "dp"))
    out_specs = (P("tensor", "dp"), P("tensor", "dp"))
    return jax.shard_map(
        per_device, mesh=mesh, in_specs=in_specs, out_specs=out_specs, check_vma=False
    )
```

time: 114 us -> 104 us (0.912)
  Pallas kernels: 107 us -> 101 us
  local copies, waits for them, and re-layouts: 5.55 us -> 1.92 us
    pallas_call x1, Pallas kernels: 107 us -> 101 us  [per_device(): pl.pallas_call(kernel, out_shape=(jax.ShapeDtypeStruct((2 * tokens, hidde...]
    unnamed x10 -> x2, local copies, waits for them, and re-layouts: 5.55 us -> 1.92 us
where the time goes in v2:
time: 104 us; the launch traced here: 103 us
  Pallas kernels  101 us (97%)
  local copies, waits for them, and re-layouts  1.92 us (2%)
    pallas_call x1, Pallas kernels, per_device(): pl.pallas_call(kernel, out_shape=(jax.ShapeDtypeStruct((2 * tokens, hidde...  101 us

profile of v2, /device:TPU:6, one launch (start us, length us, event | category | flops | bytes accessed | tf_op | source)
XLA Modules:
  0.0 103.3 jit_solution(6259077600167062525)
XLA Ops:
  0.6 100.8 %shard_map.59 = (bf16[128,896]{1,0:T(8,128)(2,1)S(1)}, f32[512,896]{1,0:T(8,128)S(1)}) custom-call(bf16[64,512]{1,0:T(8,128)(2,1)} %x_hbm.1, s32[1,512]{1,0:T(1,128)} %bitcast.3, bf16[512,896]{1,0:T(8,128)(2,1)} %w_hbm.1, bf16[2,2,32,896]{3,2,1,0:T(8,128)(2,1)} %bitcast.2), custom_call_target="tpu_custom_call" | custom-call | tf_op jit(solution)/shard_map/pallas_call | solution.py:299
  101.4 0.7 copy.8
  102.1 1.2 %copy.9 = f32[512,896]{1,0:T(8,128)} copy(f32[512,896]{1,0:T(8,128)S(1)} %get-tuple-element.5) | data formatting | bytes 3670016

commit v3 on v2

--- a/solution.py
+++ b/solution.py
@@ -13,6 +13,7 @@
 NZ = 16
 NX = 4
 NY = 4
+FAR_FIRST = (8, 7, 9, 6, 10, 5, 11, 4, 12, 3, 13, 2, 14, 1, 15)
 PARTS = 2
 
 
@@ -40,7 +41,7 @@
 
 def kernel(
     x_hbm, sign_hbm, w_hbm, u_hbm, proj_ref, grad_ref,
-    x_ref, sign_ref, inner, recv1, send2, q, qt, w, uall, part, rbuf, sbuf,
+    x_ref, sign_ref, inner, recv1, send2, recv2, q, qt, w, uall, part, rbuf, sbuf,
     loc_sem, a1_send, a1_recv, a2_send, a2_recv,
     x_send, x_recv, y_send, y_recv, c_send, c_recv,
     ag_send, ag_recv, rs_send, rs_recv,
@@ -81,7 +82,7 @@
     def greet(device):
         pl.semaphore_signal(barrier, inc=1, device_id=device, device_id_type=MESH)
 
-    for k in range(1, NZ):
+    for k in FAR_FIRST:
         greet(z_dev(k))
     for k in range(1, NX):
         greet(x_dev(k))
@@ -122,7 +123,7 @@
             device_id=partner, device_id_type=MESH,
         ).wait_recv()
 
-    for k in range(1, NZ):
+    for k in FAR_FIRST:
         j = lax.rem(me + k, NZ)
         send(inner.at[j], recv1.at[me], a1_send.at[k], a1_recv.at[k], z_dev(k))
 
@@ -152,23 +153,19 @@
     for s in range(NZ):
         send2[s] = (rotated[s] * factor).astype(BF16)
 
-    block = lax.div(me, 4)
-    tile = q.at[
-        core, lax.div(block, 2), yy, xx,
-        pl.ds(pl.multiple_of(lax.rem(block, 2) * 16, 16), 16),
-        pl.ds(pl.multiple_of(lax.rem(me, 4) * 128, 128), 128),
-    ]
+    for k in FAR_FIRST:
+        j = lax.rem(me + k, NZ)
+        send(send2.at[j], recv2.at[me], a2_send.at[k], a2_recv.at[k], z_dev(k))
+
+    gather_step(1)
+
+    recv2[me] = send2[me]
     for k in range(1, NZ):
-        j = lax.rem(me + k, NZ)
-        send(send2.at[j], tile, a2_send.at[k], a2_recv.at[k], z_dev(k))
-    own_tile = pltpu.make_async_copy(send2.at[me], tile, loc_sem.at[3])
-    own_tile.start()
-
-    gather_step(1)
-
-    own_tile.wait()
-    for k in range(1, NZ):
-        arrived(send2.at[0], a2_recv.at[k])
+        arrived(recv2.at[lax.rem(me - k + NZ, NZ)], a2_recv.at[k])
+    for j in range(NZ):
+        a, g = j // 4, j % 4
+        row = a % 2 * 16
+        q[core, a // 2, yy, xx, row : row + 16, g * 128 : (g + 1) * 128] = recv2[j]
 
     def x_from(k):
         return lax.rem(xx - k + NX, NX)
@@ -307,6 +304,7 @@
         scratch_shapes=[
             pltpu.VMEM((tokens, width), BF16),
             pltpu.VMEM((1, width), jnp.int32),
+            pltpu.VMEM((16, 16, 128), BF16),
             pltpu.VMEM((16, 16, 128), BF16),
             pltpu.VMEM((16, 16, 128), BF16),
             pltpu.VMEM((16, 16, 128), BF16),

time: 104 us -> 101 us (0.971)
  Pallas kernels: 101 us -> 98.7 us
    pallas_call x1, Pallas kernels: 101 us -> 98.7 us  [per_device(): pl.pallas_call(kernel, out_shape=(jax.ShapeDtypeStruct((2 * tokens, hidde...]
where the time goes in v3:
time: 101 us
  Pallas kernels  98.7 us (98%)
  local copies, waits for them, and re-layouts  1.92 us (2%)
    pallas_call x1, Pallas kernels, per_device(): pl.pallas_call(kernel, out_shape=(jax.ShapeDtypeStruct((2 * tokens, hidde...  98.7 us

profile of v3, /device:TPU:6, one launch (start us, length us, event | category | flops | bytes accessed | tf_op | source)
XLA Modules:
  0.0 101.2 jit_solution(12382126063447028989)
XLA Ops:
  0.6 98.7 %shard_map.59 = (bf16[128,896]{1,0:T(8,128)(2,1)S(1)}, f32[512,896]{1,0:T(8,128)S(1)}) custom-call(bf16[64,512]{1,0:T(8,128)(2,1)} %x_hbm.1, s32[1,512]{1,0:T(1,128)} %bitcast.3, bf16[512,896]{1,0:T(8,128)(2,1)} %w_hbm.1, bf16[2,2,32,896]{3,2,1,0:T(8,128)(2,1)} %bitcast.2), custom_call_target="tpu_custom_call" | custom-call | tf_op jit(solution)/shard_map/pallas_call | solution.py:296
  99.3 0.7 copy.8
  100.0 1.2 %copy.9 = f32[512,896]{1,0:T(8,128)} copy(f32[512,896]{1,0:T(8,128)S(1)} %get-tuple-element.5) | data formatting | bytes 3670016

commit v4 on v3

--- a/solution.py
+++ b/solution.py
@@ -69,14 +69,6 @@
     x_copy.start()
     sign_copy = pltpu.make_async_copy(sign_hbm, sign_ref, loc_sem.at[5])
     sign_copy.start()
-    w_copy = pltpu.make_async_copy(w_hbm, w, loc_sem.at[0])
-    w_copy.start()
-    u_copies = []
-    for h in range(2):
-        cp = pltpu.make_async_copy(u_hbm.at[h], uall.at[h, :, me], loc_sem.at[1 + h])
-        cp.start()
-        u_copies.append(cp)
-
     barrier = pltpu.get_barrier_semaphore()
 
     def greet(device):
@@ -144,6 +136,14 @@
                     )
 
     gather_step(0)
+    w_copy = pltpu.make_async_copy(w_hbm, w, loc_sem.at[0])
+    w_copy.start()
+    u_copies = []
+    for h in range(2):
+        cp = pltpu.make_async_copy(u_hbm.at[h], uall.at[h, :, me], loc_sem.at[1 + h])
+        cp.start()
+        u_copies.append(cp)
+
 
     recv1[me] = inner[me]
     for k in range(1, NZ):
@@ -258,15 +258,20 @@
     reduce_step(0)
     gather_step(6)
     reduce_step(1)
+    reduce_step(2)
     gather_step(7)
-    reduce_step(2)
+    reduce_step(3)
+    reduce_step(4)
     gather_step(8)
     for cp in u_copies:
         cp.wait()
-    for s in range(3, 8):
-        reduce_step(s)
-        if s < 7:
-            grad_tile(s - 3)
+    reduce_step(5)
+    grad_tile(0)
+    reduce_step(6)
+    grad_tile(1)
+    grad_tile(2)
+    reduce_step(7)
+    grad_tile(3)
 
     for h in range(2):
         for p in range(PARTS):

time: 101 us -> 101 us (level)
  no operation moved by 1% of the time
where the time goes in v4:
time: 101 us
  Pallas kernels  98.7 us (98%)
  local copies, waits for them, and re-layouts  1.92 us (2%)
    pallas_call x1, Pallas kernels, per_device(): pl.pallas_call(kernel, out_shape=(jax.ShapeDtypeStruct((2 * tokens, hidde...  98.7 us

profile of v4, /device:TPU:6, one launch (start us, length us, event | category | flops | bytes accessed | tf_op | source)
XLA Modules:
  0.0 101.2 jit_solution(15747988283726725458)
XLA Ops:
  0.6 98.7 %shard_map.59 = (bf16[128,896]{1,0:T(8,128)(2,1)S(1)}, f32[512,896]{1,0:T(8,128)S(1)}) custom-call(bf16[64,512]{1,0:T(8,128)(2,1)} %x_hbm.1, s32[1,512]{1,0:T(1,128)} %bitcast.3, bf16[512,896]{1,0:T(8,128)(2,1)} %w_hbm.1, bf16[2,2,32,896]{3,2,1,0:T(8,128)(2,1)} %bitcast.2), custom_call_target="tpu_custom_call" | custom-call | tf_op jit(solution)/shard_map/pallas_call | solution.py:301
  99.3 0.7 copy.8
  100.0 1.2 %copy.9 = f32[512,896]{1,0:T(8,128)} copy(f32[512,896]{1,0:T(8,128)S(1)} %get-tuple-element.5) | data formatting | bytes 3670016
